TPU v7x, 128 devices: a whole 4x4x4 slice. The times are simulated.
128 devices in a mesh: ctx: 16 (over x, y), fsdp: 8 (over z, core).
Axes of the slice: x: 4, y: 4, z: 4, core: 2. Of those that a mesh axis runs over, the one named last changes fastest.
Arguments:
- tokens: bfloat16 [16384, 4096], P(('ctx', 'fsdp')), may hold values from -360 to 360
- norm_gain: float32 [4096], replicated, may hold values from 0.1 to 1.9
- qkv_weight: bfloat16 [3, 4096, 2048], P(None, 'ctx', 'fsdp'), may hold values from -1 to 1
- out_weight: bfloat16 [2048, 4096], P('fsdp', 'ctx'), may hold values from -1 to 1
- layout: int32 [128, 16], replicated, may hold values from 0 to 127, as said below
Outputs:
- branch_out: bfloat16 [16384, 4096], P(('ctx', 'fsdp'))
Inputs may be any that keep to these rules, and one draw needn't show every extreme that they name: `layout`: every entry of query block i names a block of 0 to i. With the blocks taken in spans of 8, the query blocks of one span name at most 2 distinct blocks of any other span, and some pair of spans reaches 2 in every draw.
All inputs are finite; a program needn't handle non-finite values.
Results may differ from a plain program's by a relative error of at most 0.015.
Values may be sent and summed in bfloat16 or wider, within the bound.
A program may use at most 128 MiB of HBM per device.

v0:
```python
import math
import jax
import jax.numpy as jnp
from jax import lax
from jax.sharding import PartitionSpec as P

HEAD_DIM = 128
BLK = 128
SUMMARY = 16
EPSILON = 1e-05


def normalize(tokens, norm_gain):
    features = tokens.astype(jnp.float32)
    mean_square = jnp.mean(features * features, axis=-1, keepdims=True)
    return (features * lax.rsqrt(mean_square + EPSILON) * norm_gain).astype(jnp.bfloat16)


def shards(tokens, norm_gain, qkv_weight, out_weight, layout):
    normed = normalize(tokens, norm_gain)
    gathered = lax.all_gather(normed, "fsdp", axis=0, tiled=True)
    span_rows = gathered.shape[0]
    local_width = qkv_weight.shape[2]
    heads_here = local_width // HEAD_DIM
    projected = jnp.einsum(
        "td,cdi->cti",
        gathered,
        lax.all_gather(qkv_weight, "ctx", axis=1, tiled=True),
        preferred_element_type=jnp.float32,
    ).astype(jnp.bfloat16)
    queries, key_rows, value_rows = (projected[0], projected[1], projected[2])
    ctx_index = lax.axis_index("ctx")
    span_blocks = span_rows // BLK
    key_slots = 2 + SUMMARY
    first_block = ctx_index * span_blocks
    own_blocks = first_block + jnp.arange(span_blocks, dtype=jnp.int32)
    listed = lax.dynamic_slice_in_dim(layout, first_block, span_blocks, 0)
    key_index = jnp.concatenate([own_blocks[:, None], own_blocks[:, None] - 1, listed], axis=1)
    every_key, every_value = (
        lax.all_gather(key_rows, "ctx", axis=0, tiled=True),
        lax.all_gather(value_rows, "ctx", axis=0, tiled=True),
    )
    total_blocks = every_key.shape[0] // BLK
    pool_keys = every_key.reshape(total_blocks, BLK, local_width)
    pool_values = every_value.reshape(total_blocks, BLK, local_width)
    gather_index = jnp.maximum(key_index, 0)
    group_size = math.gcd(span_blocks, max(1, 512 // BLK))
    group_count = span_blocks // group_size
    score_scale = HEAD_DIM ** (-0.5)
    offsets = jnp.arange(BLK, dtype=jnp.int32)

    def attend(packed):
        group_queries, group_index, group_slots, group_blocks = packed
        key_blocks = pool_keys[group_index].reshape(
            group_size, key_slots, BLK, heads_here, HEAD_DIM
        )
        value_blocks = pool_values[group_index].reshape(
            group_size, key_slots, BLK, heads_here, HEAD_DIM
        )
        scores = (
            jnp.einsum(
                "bqhd,bnkhd->bhqnk", group_queries, key_blocks, preferred_element_type=jnp.float32
            )
            * score_scale
        )
        query_pos = group_blocks[:, None] * BLK + offsets[None, :]
        key_pos = group_slots[:, :, None] * BLK + offsets[None, None, :]
        allowed = (key_pos[:, None, :, :] <= query_pos[:, :, None, None]) & (
            key_pos[:, None, :, :] >= 0
        )
        allowed = allowed[:, None]
        scores = jnp.where(allowed, scores, -1e30)
        row_max = jnp.max(scores, axis=(3, 4), keepdims=True)
        weights = jnp.where(allowed, jnp.exp(scores - row_max), 0.0)
        denominator = jnp.sum(weights, axis=(3, 4), keepdims=True)
        weights = (weights / denominator).astype(jnp.bfloat16)
        blended = jnp.einsum(
            "bhqnk,bnkhd->bqhd", weights, value_blocks, preferred_element_type=jnp.float32
        )
        return blended.astype(jnp.bfloat16)

    packed_inputs = (
        queries.reshape(group_count, group_size, BLK, heads_here, HEAD_DIM),
        gather_index.reshape(group_count, group_size, key_slots),
        key_index.reshape(group_count, group_size, key_slots),
        own_blocks.reshape(group_count, group_size),
    )
    blended_all = lax.map(attend, packed_inputs)
    attended = blended_all.reshape(span_rows, local_width)
    projection = lax.all_gather(out_weight, "ctx", axis=1, tiled=True)
    return lax.psum_scatter(
        jnp.dot(attended, projection, preferred_element_type=jnp.float32).astype(jnp.bfloat16),
        "fsdp",
        scatter_dimension=0,
        tiled=True,
    )


def solution(mesh):
    placed = (P(("ctx", "fsdp"), None), P(), P(None, "ctx", "fsdp"), P("fsdp", "ctx"), P())
    return jax.shard_map(
        shards, mesh=mesh, in_specs=placed, out_specs=P(("ctx", "fsdp"), None), check_vma=False
    )
```

profile of v0, /device:TPU:1, one launch (start us, length us, event | category | flops | bytes accessed | tf_op | source)
XLA Modules:
  0.0 463.3 jit_solution(6775085235407852516)
XLA Ops:
  7.3 1.5 fusion.24
  8.8 2.5 fusion.26
  11.4 62.3 %all-gather.10.cloned.1.call-done = bf16[3,4096,256]{2,1,0:T(8,128)(2,1)} async-done(((bf16[3,256,256]{2,1,0:T(8,128)(2,1)}), bf16[3,4096,256]{2,1,0:T(8,128)(2,1)}) %all-gather.10.cloned.1.call-update) | async-done | bytes 6291472 | tf_op jit(solution)/shard_map/all_gather | solution.py:28
  73.7 51.9 %all-gather.8.cloned.1.call-done = bf16[1024,4096]{1,0:T(8,128)(2,1)} async-done(((bf16[128,4096]{1,0:T(8,128)(2,1)}), bf16[1024,4096]{1,0:T(8,128)(2,1)}) %all-gather.8.cloned.1.call-update) | async-done | bytes 8388624 | tf_op jit(solution)/shard_map/all_gather | solution.py:21
  125.6 10.9 %fusion.30 = bf16[3,1024,256]{2,1,0:T(8,128)(2,1)S(1)} fusion(bf16[3,4096,256]{2,1,0:T(8,128)(2,1)} %all-gather.10.cloned.1.call-done, bf16[1024,4096]{1,0:T(8,128)(2,1)} %all-gather.8.cloned.1.call-done), kind=kOutput, calls=%fused_computation.40 | convolution fusion | flops 6443237376 | bytes 16252928 | tf_op jit(solution)/shard_map/td,cdi->cti/dot_general | solution.py:25
  139.3 68.6 %all-gather.14.cloned.1.call-done = bf16[1,16384,256]{2,1,0:T(8,128)(2,1)} async-done(((bf16[1,1024,256]{2,1,0:T(8,128)(2,1)}), bf16[1,16384,256]{2,1,0:T(8,128)(2,1)}) %all-gather.14.cloned.1.call-update) | async-done | bytes 8388624 | tf_op jit(solution)/shard_map/all_gather | solution.py:41
  207.9 72.4 %all-gather.16.cloned.1.call-done = bf16[1,16384,256]{2,1,0:T(8,128)(2,1)} async-done(((bf16[1,1024,256]{2,1,0:T(8,128)(2,1)}), bf16[1,16384,256]{2,1,0:T(8,128)(2,1)}) %all-gather.16.cloned.1.call-update) | async-done | bytes 8388624 | tf_op jit(solution)/shard_map/all_gather | solution.py:40
  280.3 116.7 %while.12 = (s32[]{:T(128)}, bf16[2,4,128,2,128]{4,3,2,1,0:T(2,128)(2,1)S(1)}, s32[2,4,18]{2,1,0:T(4,128)S(1)}, bf16[128,128,256]{2,1,0:T(8,128)(2,1)}, s32[2,4,...) while((s32[]{:T(128)}, ...), condition=%wide.region_4.5_spmd.clone.clone, body=%wide.region_1.4_spmd.clone.clone.sunk | while | flops 1243507456 | bytes 139060496 | solution.py:88
  280.6 3.5 compare_and_fusion.2
  284.2 8.9 %gather_fusion = bf16[72,128,256]{2,1,0:T(8,128)(2,1)} fusion(bf16[128,128,256]{2,1,0:T(8,128)(2,1)} %get-tuple-element.209, s32[1024]{0:T(1024)S(1)} %pad_clamp_fusion.2), kind=kCustom, calls=%fused_computation.1.clone.clone.1 | custom fusion | bytes 9437472 | tf_op jit(solution)/shard_map/while/body/eval_jaxpr/gather | solution.py:54
  293.1 7.7 %reshape.196 = bf16[4,18,128,2,128]{4,3,2,1,0:T(2,128)(2,1)} reshape(bf16[72,128,256]{2,1,0:T(8,128)(2,1)} %gather_fusion) | data formatting | bytes 9437184 | tf_op jit(solution)/shard_map/while/body/eval_jaxpr/reshape | solution.py:54
  300.8 3.6 copy.44
  304.6 1.4 fusion.48
  306.0 1.6 fusion.50
  307.6 2.1 copy-done.2
  309.7 2.5 fusion.51
  312.2 9.0 %gather_fusion.1 = bf16[72,128,256]{2,1,0:T(8,128)(2,1)} fusion(bf16[128,128,256]{2,1,0:T(8,128)(2,1)} %get-tuple-element.205, s32[1024]{0:T(1024)S(1)} %pad_clamp_fusion.2), kind=kCustom, calls=%fused_computation.clone.clone.1 | custom fusion | bytes 9437472 | tf_op jit(solution)/shard_map/while/body/eval_jaxpr/gather | solution.py:57
  321.2 7.7 %reshape.197 = bf16[4,18,128,2,128]{4,3,2,1,0:T(2,128)(2,1)} reshape(bf16[72,128,256]{2,1,0:T(8,128)(2,1)} %gather_fusion.1) | data formatting | bytes 9437184 | tf_op jit(solution)/shard_map/while/body/eval_jaxpr/reshape | solution.py:57
  328.9 9.4 %fusion.52 = bf16[1,4,128,2,128]{2,4,3,1,0:T(8,128)(2,1)S(1)} fusion(f32[4,2,128,18,128]{2,4,3,1,0:T(8,128)} %bitcast.66, f32[4,2,128]{2,1,0:T(2,128)S(1)} %fusion.51, f32[4,2,128]{2,1,0:T(2,128)S(1)} %fusion.50, pred[4,128,18,128]{1,3,2,0:T(8,128)(4,1)S(1)} %compare_and_fusion.2, bf16[4,18,128,2,128]{4,3,2,1,0:T(2,128)(2,1)} %reshape.197), kind=kOutput, calls=%fused_computation.14.clone.1 | convolution fusion | flops 618266624 | bytes 15605760 | tf_op jit(solution)/shard_map/while/body/eval_jaxpr/bhqnk,bnkhd->bqhd/dot_general | solution.py:77
  339.0 3.5 compare_and_fusion.2
  342.6 8.8 %gather_fusion = bf16[72,128,256]{2,1,0:T(8,128)(2,1)} fusion(bf16[128,128,256]{2,1,0:T(8,128)(2,1)} %get-tuple-element.209, s32[1024]{0:T(1024)S(1)} %pad_clamp_fusion.2), kind=kCustom, calls=%fused_computation.1.clone.clone.1 | custom fusion | bytes 9437472 | tf_op jit(solution)/shard_map/while/body/eval_jaxpr/gather | solution.py:54
  351.4 7.7 %reshape.196 = bf16[4,18,128,2,128]{4,3,2,1,0:T(2,128)(2,1)} reshape(bf16[72,128,256]{2,1,0:T(8,128)(2,1)} %gather_fusion) | data formatting | bytes 9437184 | tf_op jit(solution)/shard_map/while/body/eval_jaxpr/reshape | solution.py:54
  359.2 3.6 copy.44
  362.9 1.4 fusion.48
  364.4 1.6 fusion.50
  365.9 2.1 copy-done.2
  368.0 2.5 fusion.51
  370.5 8.8 %gather_fusion.1 = bf16[72,128,256]{2,1,0:T(8,128)(2,1)} fusion(bf16[128,128,256]{2,1,0:T(8,128)(2,1)} %get-tuple-element.205, s32[1024]{0:T(1024)S(1)} %pad_clamp_fusion.2), kind=kCustom, calls=%fused_computation.clone.clone.1 | custom fusion | bytes 9437472 | tf_op jit(solution)/shard_map/while/body/eval_jaxpr/gather | solution.py:57
  379.3 7.7 %reshape.197 = bf16[4,18,128,2,128]{4,3,2,1,0:T(2,128)(2,1)} reshape(bf16[72,128,256]{2,1,0:T(8,128)(2,1)} %gather_fusion.1) | data formatting | bytes 9437184 | tf_op jit(solution)/shard_map/while/body/eval_jaxpr/reshape | solution.py:57
  387.1 9.4 %fusion.52 = bf16[1,4,128,2,128]{2,4,3,1,0:T(8,128)(2,1)S(1)} fusion(f32[4,2,128,18,128]{2,4,3,1,0:T(8,128)} %bitcast.66, f32[4,2,128]{2,1,0:T(2,128)S(1)} %fusion.51, f32[4,2,128]{2,1,0:T(2,128)S(1)} %fusion.50, pred[4,128,18,128]{1,3,2,0:T(8,128)(4,1)S(1)} %compare_and_fusion.2, bf16[4,18,128,2,128]{4,3,2,1,0:T(2,128)(2,1)} %reshape.197), kind=kOutput, calls=%fused_computation.14.clone.1 | convolution fusion | flops 618266624 | bytes 15605760 | tf_op jit(solution)/shard_map/while/body/eval_jaxpr/bhqnk,bnkhd->bqhd/dot_general | solution.py:77
  397.1 7.2 %convolution_convert_fusion = bf16[1024,4096]{1,0:T(8,128)(2,1)} fusion(bf16[256,4096]{1,0:T(8,128)(2,1)} %all-gather.12.cloned.1.call-done, bf16[128,8,2,128]{3,2,1,0:T(2,128)(2,1)S(1)} %bitcast.70), kind=kOutput, calls=%fused_computation.33 | convolution fusion | flops 2151677952 | bytes 11010048 | tf_op jit(solution)/shard_map/dot_general | solution.py:92
  404.3 52.1 %reduce-scatter.2.cloned.1.call-done = bf16[128,4096]{1,0:T(8,128)(2,1)} async-done(((bf16[1024,4096]{1,0:T(8,128)(2,1)}), bf16[128,4096]{1,0:T(8,128)(2,1)}) %reduce-scatter.2.cloned.1.call-update) | async-done | bytes 1048592 | tf_op jit(solution)/shard_map/reduce_scatter | solution.py:91
  (50 shorter events, 5.4 us)
Async XLA Ops:
  6.5 132.4 %copy-start = (s32[128,16]{0,1:T(8,128)S(1)}, s32[128,16]{0,1:T(8,128)}, u32[]{:S(2)}) copy-start(s32[128,16]{0,1:T(8,128)} %param.11) | copy-start | bytes 24580
  6.5 67.2 %all-gather.10.cloned.1.call-start = ((), (), s32[]{:S(2)}) async-start(), calls=%async_computation.2 | async-start | bytes 6684672 | tf_op jit(solution)/shard_map/all_gather | solution.py:28
  7.3 118.4 %all-gather.8.cloned.1.call-start = ((), (), s32[]{:S(2)}) async-start(), calls=%async_computation.1 | async-start | bytes 9437184 | tf_op jit(solution)/shard_map/all_gather | solution.py:21
  11.4 196.5 %all-gather.14.cloned.1.call-start = ((), (), s32[]{:S(2)}) async-start(), calls=%async_computation.5 | async-start | bytes 8912896 | tf_op jit(solution)/shard_map/all_gather | solution.py:41
  137.7 142.7 %all-gather.16.cloned.1.call-start = ((), (), s32[]{:S(2)}) async-start(), calls=%async_computation.6 | async-start | bytes 8912896 | tf_op jit(solution)/shard_map/all_gather | solution.py:40
  138.2 258.9 %all-gather.12.cloned.1.call-start = ((), (), s32[]{:S(2)}) async-start(), calls=%async_computation.3 | async-start | bytes 2228224 | tf_op jit(solution)/shard_map/all_gather | solution.py:90
  138.8 317.6 %reduce-scatter.2.cloned.1.call-start = ((), (), s32[]{:S(2)}) async-start(), calls=%async_computation.4 | async-start | bytes 9437184 | tf_op jit(solution)/shard_map/reduce_scatter | solution.py:91
  306.0 3.6 copy-start.2
  364.3 3.7 copy-start.2
  397.1 59.3 %copy-start.1 = (s32[128,16]{0,1:T(8,128)S(1)}, s32[128,16]{0,1:T(8,128)}, u32[]{:S(2)}) copy-start(s32[128,16]{0,1:T(8,128)} %param.11) | copy-start | bytes 24580
Sparse Core Ops, SparseCore 0:
  9.5 64.1 all-gather.9
  75.4 50.1 all-gather.7
  137.8 70.0 all-gather.13
  209.9 70.3 all-gather.15
  282.3 45.1 all-gather.11
  404.4 51.9 reduce-scatter.1
where the time goes:
time: 464 us; the launch traced here: 463 us
  waiting for transfers between devices  309 us (67%)
  local copies, waits for them, and re-layouts  80.4 us (17%)
  matrix products  39.6 us (9%)
  other arithmetic  19.8 us (4%)
  between operations  13.5 us (3%)
    all_gather x1, waiting for transfers between devices, shards(): lax.all_gather(key_rows, 'ctx', axis=0, tiled=True)  72.4 us
    all_gather x1, waiting for transfers between devices, shards(): lax.all_gather(value_rows, 'ctx', axis=0, tiled=True)  68.6 us
    all_gather x1, waiting for transfers between devices, shards(): lax.all_gather(qkv_weight, 'ctx', axis=1, tiled=True)  62.3 us
    reduce_scatter x1, waiting for transfers between devices, shards(): lax.psum_scatter(jnp.dot(attended, projection, preferred_element_type=jnp...  52.1 us
    all_gather x1, waiting for transfers between devices, shards(): gathered = lax.all_gather(normed, 'fsdp', axis=0, tiled=True)  51.9 us
    reshape x4, local copies, waits for them, and re-layouts, attend(): pool_keys[group_index]  22.6 us
    dot_general x2, matrix products, attend(): jnp.einsum('bhqnk,bnkhd->bqhd', weights, value_blocks, preferred_element_...  18.8 us
    gather x2, local copies, waits for them, and re-layouts, attend(): pool_values[group_index]  17.8 us
  transfers between devices with their start and end apart: 6, of which 5 were waited for; matrix products, arithmetic and copies ran while one was open for 25% of the time, Pallas kernels for 0%

commit v1 on v0

--- a/solution.py
+++ b/solution.py
@@ -8,6 +8,28 @@
 BLK = 128
 SUMMARY = 16
 EPSILON = 1e-05
+
+
+def in_order(tiles, dim):
+    shape = list(tiles.shape[1:])
+    shape[dim] *= tiles.shape[0]
+    return jnp.moveaxis(tiles, 0, dim).reshape(shape)
+
+
+def ring_gather(x, axis, dim):
+    size = lax.axis_size(axis)
+    pairs = [(i, (i + 1) % size) for i in range(size)]
+    back = [(b, a) for a, b in pairs]
+    lower, upper = ([], [])
+    for hop in range(size - 1):
+        if hop % 2 == 0:
+            lower.append(lax.ppermute(lower[-1] if lower else x, axis, pairs))
+        else:
+            upper.append(lax.ppermute(upper[-1] if upper else x, axis, back))
+    tiles = jnp.stack([*lower[::-1], x, *upper])
+    shift = lax.axis_index(axis) - len(lower)
+    tiles = tiles[(jnp.arange(size) - shift) % size]
+    return in_order(tiles, dim)
 
 
 def normalize(tokens, norm_gain):
@@ -38,7 +60,7 @@
     key_index = jnp.concatenate([own_blocks[:, None], own_blocks[:, None] - 1, listed], axis=1)
     every_key, every_value = (
         lax.all_gather(key_rows, "ctx", axis=0, tiled=True),
-        lax.all_gather(value_rows, "ctx", axis=0, tiled=True),
+        ring_gather(value_rows, "ctx", 0),
     )
     total_blocks = every_key.shape[0] // BLK
     pool_keys = every_key.reshape(total_blocks, BLK, local_width)

time: 464 us -> 588 us (1.27)
  waiting for transfers between devices: 309 us -> 380 us
  starting transfers between devices: 0.2 us -> 31.2 us
  local copies, waits for them, and re-layouts: 80.4 us -> 100 us
    ppermute x0 -> x15, waiting for transfers between devices: none -> 198 us  [the longest x8 108 us: ring_gather(): lower.append(lax.ppermute(lower[-1] if lower else x, axis, pairs))]
    all_gather x1, waiting for transfers between devices: 72.4 us -> 0.01 us  [shards(): lax.all_gather(key_rows, 'ctx', axis=0, tiled=True)]
    all_gather x1 -> x0, waiting for transfers between devices: 68.6 us -> none  [shards(): lax.all_gather(value_rows, 'ctx', axis=0, tiled=True)]
    ppermute x0 -> x15, starting transfers between devices: none -> 31.1 us  [the longest x7 29.8 us: ring_gather(): upper.append(lax.ppermute(upper[-1] if upper else x, axis, back))]
    reduce_scatter x1, waiting for transfers between devices: 52.1 us -> 67.8 us  [shards(): lax.psum_scatter(jnp.dot(attended, projection, preferred_element_type=jnp...]
    unnamed x5 -> x21, local copies, waits for them, and re-layouts: 0.08 us -> 13.9 us
    gather x0 -> x1, local copies, waits for them, and re-layouts: none -> 8.42 us  [ring_gather(): tiles = tiles[(jnp.arange(size) - shift) % size]]
  transfers between devices with their start and end apart: 6 -> 20, of which waited for: 5 -> 18; matrix products, arithmetic and copies ran while one was open for 25% -> 23% of each run, Pallas kernels for 0% -> 0%
where the time goes in v1:
time: 588 us; the launch traced here: 586 us
  waiting for transfers between devices  380 us (65%)
  local copies, waits for them, and re-layouts  100 us (17%)
  matrix products  39.7 us (7%)
  starting transfers between devices  31.2 us (5%)
  other arithmetic  21.1 us (4%)
  between operations  13.2 us (2%)
    ppermute x8, waiting for transfers between devices, ring_gather(): lower.append(lax.ppermute(lower[-1] if lower else x, axis, pairs))  108 us
    ppermute x7, waiting for transfers between devices, ring_gather(): upper.append(lax.ppermute(upper[-1] if upper else x, axis, back))  89.6 us
    reduce_scatter x1, waiting for transfers between devices, shards(): lax.psum_scatter(jnp.dot(attended, projection, preferred_element_type=jnp...  67.8 us
    all_gather x1, waiting for transfers between devices, shards(): lax.all_gather(qkv_weight, 'ctx', axis=1, tiled=True)  62.3 us
    all_gather x1, waiting for transfers between devices, shards(): gathered = lax.all_gather(normed, 'fsdp', axis=0, tiled=True)  51.9 us
    ppermute x7, starting transfers between devices, ring_gather(): upper.append(lax.ppermute(upper[-1] if upper else x, axis, back))  29.8 us
    reshape x4, local copies, waits for them, and re-layouts, attend(): pool_keys[group_index]  22.6 us
    dot_general x2, matrix products, attend(): jnp.einsum('bhqnk,bnkhd->bqhd', weights, value_blocks, preferred_element_...  18.8 us
  transfers between devices with their start and end apart: 20, of which 18 were waited for; matrix products, arithmetic and copies ran while one was open for 23% of the time, Pallas kernels for 0%

profile of v1, /device:TPU:1, one launch (start us, length us, event | category | flops | bytes accessed | tf_op | source)
XLA Modules:
  0.0 586.4 jit_solution(16924199974314543804)
XLA Ops:
  11.4 62.3 %all-gather.8.cloned.1.call-done = bf16[3,4096,256]{2,1,0:T(8,128)(2,1)} async-done(((bf16[3,256,256]{2,1,0:T(8,128)(2,1)}), bf16[3,4096,256]{2,1,0:T(8,128)(2,1)}) %all-gather.8.cloned.1.call-update) | async-done | bytes 6291472 | tf_op jit(solution)/shard_map/all_gather | solution.py:50
  73.7 51.9 %all-gather.6.cloned.1.call-done = bf16[1024,4096]{1,0:T(8,128)(2,1)} async-done(((bf16[128,4096]{1,0:T(8,128)(2,1)}), bf16[1024,4096]{1,0:T(8,128)(2,1)}) %all-gather.6.cloned.1.call-update) | async-done | bytes 8388624 | tf_op jit(solution)/shard_map/all_gather | solution.py:43
  125.6 10.9 %fusion.30 = bf16[3,1024,256]{2,1,0:T(8,128)(2,1)S(1)} fusion(bf16[3,4096,256]{2,1,0:T(8,128)(2,1)} %all-gather.8.cloned.1.call-done, bf16[1024,4096]{1,0:T(8,128)(2,1)} %all-gather.6.cloned.1.call-done), kind=kOutput, calls=%fused_computation.41 | convolution fusion | flops 6443237376 | bytes 16252928 | tf_op jit(solution)/shard_map/td,cdi->cti/dot_general | solution.py:47
  137.9 15.3 %collective-permute-done = bf16[1024,256]{1,0:T(8,128)(2,1)S(1)} collective-permute-done((bf16[1024,256]{1,0:T(8,128)(2,1)S(1)}, bf16[1024,256]{1,0:T(8,128)(2,1)S(1)}, u32[]{:S(2)}, u32[]{:S(2)}) %collective-permute-start) | collective-permute-done | bytes 524320 | tf_op jit(solution)/shard_map/ppermute | solution.py:26
  153.2 15.7 %collective-permute-done.1 = bf16[1024,256]{1,0:T(8,128)(2,1)S(1)} collective-permute-done((bf16[1024,256]{1,0:T(8,128)(2,1)S(1)}, bf16[1024,256]{1,0:T(8,128)(2,1)S(1)}, u32[]{:S(2)}, u32[]{:S(2)}) %collective-permute-start.1) | collective-permute-done | bytes 524320 | tf_op jit(solution)/shard_map/ppermute | solution.py:26
  168.9 14.8 %collective-permute-done.2 = bf16[1024,256]{1,0:T(8,128)(2,1)S(1)} collective-permute-done((bf16[1024,256]{1,0:T(8,128)(2,1)S(1)}, bf16[1024,256]{1,0:T(8,128)(2,1)S(1)}, u32[]{:S(2)}, u32[]{:S(2)}) %collective-permute-start.2) | collective-permute-done | bytes 524320 | tf_op jit(solution)/shard_map/ppermute | solution.py:26
  183.7 14.0 %collective-permute-done.3 = bf16[1024,256]{1,0:T(8,128)(2,1)S(1)} collective-permute-done((bf16[1024,256]{1,0:T(8,128)(2,1)S(1)}, bf16[1024,256]{1,0:T(8,128)(2,1)S(1)}, u32[]{:S(2)}, u32[]{:S(2)}) %collective-permute-start.3) | collective-permute-done | bytes 524320 | tf_op jit(solution)/shard_map/ppermute | solution.py:26
  197.7 13.1 %collective-permute-done.4 = bf16[1024,256]{1,0:T(8,128)(2,1)S(1)} collective-permute-done((bf16[1024,256]{1,0:T(8,128)(2,1)S(1)}, bf16[1024,256]{1,0:T(8,128)(2,1)S(1)}, u32[]{:S(2)}, u32[]{:S(2)}) %collective-permute-start.4) | collective-permute-done | bytes 524320 | tf_op jit(solution)/shard_map/ppermute | solution.py:26
  210.8 12.3 %collective-permute-done.5 = bf16[1024,256]{1,0:T(8,128)(2,1)S(1)} collective-permute-done((bf16[1024,256]{1,0:T(8,128)(2,1)S(1)}, bf16[1024,256]{1,0:T(8,128)(2,1)S(1)}, u32[]{:S(2)}, u32[]{:S(2)}) %collective-permute-start.5) | collective-permute-done | bytes 524320 | tf_op jit(solution)/shard_map/ppermute | solution.py:26
  223.1 11.3 %collective-permute-done.6 = bf16[1024,256]{1,0:T(8,128)(2,1)S(1)} collective-permute-done((bf16[1024,256]{1,0:T(8,128)(2,1)S(1)}, bf16[1024,256]{1,0:T(8,128)(2,1)S(1)}, u32[]{:S(2)}, u32[]{:S(2)}) %collective-permute-start.6) | collective-permute-done | bytes 524320 | tf_op jit(solution)/shard_map/ppermute | solution.py:26
  234.5 11.5 %collective-permute-done.7 = bf16[1024,256]{1,0:T(8,128)(2,1)S(1)} collective-permute-done((bf16[1024,256]{1,0:T(8,128)(2,1)S(1)}, bf16[1024,256]{1,0:T(8,128)(2,1)S(1)}, u32[]{:S(2)}, u32[]{:S(2)}) %collective-permute-start.7) | collective-permute-done | bytes 524320 | tf_op jit(solution)/shard_map/ppermute | solution.py:26
  253.8 8.0 %collective-permute-done.8 = bf16[1024,256]{1,0:T(8,128)(2,1)S(1)} collective-permute-done((bf16[1024,256]{1,0:T(8,128)(2,1)S(1)}, bf16[1024,256]{1,0:T(8,128)(2,1)S(1)}, u32[]{:S(2)}, u32[]{:S(2)}) %collective-permute-start.8) | collective-permute-done | bytes 524320 | tf_op jit(solution)/shard_map/ppermute | solution.py:28
  265.2 16.9 %collective-permute-done.9 = bf16[1024,256]{1,0:T(8,128)(2,1)S(1)} collective-permute-done((bf16[1024,256]{1,0:T(8,128)(2,1)S(1)}, bf16[1024,256]{1,0:T(8,128)(2,1)S(1)}, u32[]{:S(2)}, u32[]{:S(2)}) %collective-permute-start.9) | collective-permute-done | bytes 524320 | tf_op jit(solution)/shard_map/ppermute | solution.py:28
  287.1 7.8 %collective-permute-done.10 = bf16[1024,256]{1,0:T(8,128)(2,1)S(1)} collective-permute-done((bf16[1024,256]{1,0:T(8,128)(2,1)S(1)}, bf16[1024,256]{1,0:T(8,128)(2,1)S(1)}, u32[]{:S(2)}, u32[]{:S(2)}) %collective-permute-start.10) | collective-permute-done | bytes 524320 | tf_op jit(solution)/shard_map/ppermute | solution.py:28
  299.8 17.8 %collective-permute-done.11 = bf16[1024,256]{1,0:T(8,128)(2,1)S(1)} collective-permute-done((bf16[1024,256]{1,0:T(8,128)(2,1)S(1)}, bf16[1024,256]{1,0:T(8,128)(2,1)S(1)}, u32[]{:S(2)}, u32[]{:S(2)}) %collective-permute-start.11) | collective-permute-done | bytes 524320 | tf_op jit(solution)/shard_map/ppermute | solution.py:28
  323.4 20.4 %collective-permute-done.12 = bf16[1024,256]{1,0:T(8,128)(2,1)} collective-permute-done((bf16[1024,256]{1,0:T(8,128)(2,1)S(1)}, bf16[1024,256]{1,0:T(8,128)(2,1)}, u32[]{:S(2)}, u32[]{:S(2)}) %collective-permute-start.12) | collective-permute-done | bytes 524320 | tf_op jit(solution)/shard_map/ppermute | solution.py:28
  343.8 5.6 collective-permute-start.13
  350.8 14.0 %collective-permute-done.13 = bf16[1024,256]{1,0:T(8,128)(2,1)} collective-permute-done((bf16[1024,256]{1,0:T(8,128)(2,1)}, bf16[1024,256]{1,0:T(8,128)(2,1)}, u32[]{:S(2)}, u32[]{:S(2)}) %collective-permute-start.13) | collective-permute-done | bytes 524320 | tf_op jit(solution)/shard_map/ppermute | solution.py:28
  383.9 8.4 %gather_fusion.2 = bf16[16,1024,256]{2,1,0:T(8,128)(2,1)} fusion(bf16[16,1024,256]{2,1,0:T(8,128)(2,1)} %bitcast_dynamic-update-slice_fusion, s32[1024]{0:T(1024)} %pad_clamp_fusion.1), kind=kCustom, calls=%fused_computation.2 | custom fusion | bytes 16777280 | tf_op jit(solution)/shard_map/gather | solution.py:31
  392.3 112.4 %while.12 = (s32[]{:T(128)}, bf16[2,4,128,2,128]{4,3,2,1,0:T(2,128)(2,1)S(1)}, s32[2,4,18]{2,1,0:T(4,128)S(1)}, bf16[128,128,256]{2,1,0:T(8,128)(2,1)}, s32[2,4,...) while((s32[]{:T(128)}, ...), condition=%wide.region_4.5_spmd.clone.clone, body=%wide.region_1.4_spmd.clone.clone.sunk | while | flops 1243507456 | bytes 139060496 | solution.py:110
  396.2 8.9 %gather_fusion = bf16[72,128,256]{2,1,0:T(8,128)(2,1)} fusion(bf16[128,128,256]{2,1,0:T(8,128)(2,1)} %get-tuple-element.209, s32[1024]{0:T(1024)S(1)} %pad_clamp_fusion.3), kind=kCustom, calls=%fused_computation.1.clone.clone.1 | custom fusion | bytes 9437472 | tf_op jit(solution)/shard_map/while/body/eval_jaxpr/gather | solution.py:76
  405.1 7.7 %reshape.247 = bf16[4,18,128,2,128]{4,3,2,1,0:T(2,128)(2,1)} reshape(bf16[72,128,256]{2,1,0:T(8,128)(2,1)} %gather_fusion) | data formatting | bytes 9437184 | tf_op jit(solution)/shard_map/while/body/eval_jaxpr/reshape | solution.py:76
  422.1 8.9 %gather_fusion.1 = bf16[72,128,256]{2,1,0:T(8,128)(2,1)} fusion(bf16[128,128,256]{2,1,0:T(8,128)(2,1)} %get-tuple-element.205, s32[1024]{0:T(1024)S(1)} %pad_clamp_fusion.3), kind=kCustom, calls=%fused_computation.clone.clone.1 | custom fusion | bytes 9437472 | tf_op jit(solution)/shard_map/while/body/eval_jaxpr/gather | solution.py:79
  431.0 7.7 %reshape.248 = bf16[4,18,128,2,128]{4,3,2,1,0:T(2,128)(2,1)} reshape(bf16[72,128,256]{2,1,0:T(8,128)(2,1)} %gather_fusion.1) | data formatting | bytes 9437184 | tf_op jit(solution)/shard_map/while/body/eval_jaxpr/reshape | solution.py:79
  438.7 9.4 %fusion.54 = bf16[1,4,128,2,128]{2,4,3,1,0:T(8,128)(2,1)S(1)} fusion(f32[4,2,128,18,128]{2,4,3,1,0:T(8,128)} %bitcast.100, f32[4,2,128]{2,1,0:T(2,128)S(1)} %fusion.53, f32[4,2,128]{2,1,0:T(2,128)S(1)} %fusion.52, pred[4,128,18,128]{1,3,2,0:T(8,128)(4,1)S(1)} %compare_and_fusion.2, bf16[4,18,128,2,128]{4,3,2,1,0:T(2,128)(2,1)} %reshape.248), kind=kOutput, calls=%fused_computation.15.clone.1 | convolution fusion | flops 618266624 | bytes 15605760 | tf_op jit(solution)/shard_map/while/body/eval_jaxpr/bhqnk,bnkhd->bqhd/dot_general | solution.py:99
  452.4 8.9 %gather_fusion = bf16[72,128,256]{2,1,0:T(8,128)(2,1)} fusion(bf16[128,128,256]{2,1,0:T(8,128)(2,1)} %get-tuple-element.209, s32[1024]{0:T(1024)S(1)} %pad_clamp_fusion.3), kind=kCustom, calls=%fused_computation.1.clone.clone.1 | custom fusion | bytes 9437472 | tf_op jit(solution)/shard_map/while/body/eval_jaxpr/gather | solution.py:76
  461.2 7.7 %reshape.247 = bf16[4,18,128,2,128]{4,3,2,1,0:T(2,128)(2,1)} reshape(bf16[72,128,256]{2,1,0:T(8,128)(2,1)} %gather_fusion) | data formatting | bytes 9437184 | tf_op jit(solution)/shard_map/while/body/eval_jaxpr/reshape | solution.py:76
  478.2 8.8 %gather_fusion.1 = bf16[72,128,256]{2,1,0:T(8,128)(2,1)} fusion(bf16[128,128,256]{2,1,0:T(8,128)(2,1)} %get-tuple-element.205, s32[1024]{0:T(1024)S(1)} %pad_clamp_fusion.3), kind=kCustom, calls=%fused_computation.clone.clone.1 | custom fusion | bytes 9437472 | tf_op jit(solution)/shard_map/while/body/eval_jaxpr/gather | solution.py:79
  487.0 7.7 %reshape.248 = bf16[4,18,128,2,128]{4,3,2,1,0:T(2,128)(2,1)} reshape(bf16[72,128,256]{2,1,0:T(8,128)(2,1)} %gather_fusion.1) | data formatting | bytes 9437184 | tf_op jit(solution)/shard_map/while/body/eval_jaxpr/reshape | solution.py:79
  494.8 9.4 %fusion.54 = bf16[1,4,128,2,128]{2,4,3,1,0:T(8,128)(2,1)S(1)} fusion(f32[4,2,128,18,128]{2,4,3,1,0:T(8,128)} %bitcast.100, f32[4,2,128]{2,1,0:T(2,128)S(1)} %fusion.53, f32[4,2,128]{2,1,0:T(2,128)S(1)} %fusion.52, pred[4,128,18,128]{1,3,2,0:T(8,128)(4,1)S(1)} %compare_and_fusion.2, bf16[4,18,128,2,128]{4,3,2,1,0:T(2,128)(2,1)} %reshape.248), kind=kOutput, calls=%fused_computation.15.clone.1 | convolution fusion | flops 618266624 | bytes 15605760 | tf_op jit(solution)/shard_map/while/body/eval_jaxpr/bhqnk,bnkhd->bqhd/dot_general | solution.py:99
  504.8 7.2 %convolution_convert_fusion = bf16[1024,4096]{1,0:T(8,128)(2,1)} fusion(bf16[256,4096]{1,0:T(8,128)(2,1)} %all-gather.10.cloned.1.call-done, bf16[128,8,2,128]{3,2,1,0:T(2,128)(2,1)S(1)} %bitcast.104), kind=kOutput, calls=%fused_computation.34 | convolution fusion | flops 2151677952 | bytes 11010048 | tf_op jit(solution)/shard_map/dot_general | solution.py:114
  512.1 67.8 %reduce-scatter.2.cloned.1.call-done = bf16[128,4096]{1,0:T(8,128)(2,1)} async-done(((bf16[1024,4096]{1,0:T(8,128)(2,1)}), bf16[128,4096]{1,0:T(8,128)(2,1)}) %reduce-scatter.2.cloned.1.call-update) | async-done | bytes 1048592 | tf_op jit(solution)/shard_map/reduce_scatter | solution.py:113
  (98 shorter events, 80.5 us)
Async XLA Ops:
  6.5 316.7 %copy-start = (s32[128,16]{0,1:T(8,128)S(1)}, s32[128,16]{0,1:T(8,128)}, u32[]{:S(2)}) copy-start(s32[128,16]{0,1:T(8,128)} %param.11) | copy-start | bytes 24580
  6.5 67.2 %all-gather.8.cloned.1.call-start = ((), (), s32[]{:S(2)}) async-start(), calls=%async_computation.2 | async-start | bytes 6684672 | tf_op jit(solution)/shard_map/all_gather | solution.py:50
  7.3 118.4 %all-gather.6.cloned.1.call-start = ((), (), s32[]{:S(2)}) async-start(), calls=%async_computation.1 | async-start | bytes 9437184 | tf_op jit(solution)/shard_map/all_gather | solution.py:43
  11.4 380.9 %all-gather.12.cloned.1.call-start = ((), (), s32[]{:S(2)}) async-start(), calls=%async_computation.5 | async-start | bytes 8912896 | tf_op jit(solution)/shard_map/all_gather | solution.py:62
  136.6 16.6 %collective-permute-start = (bf16[1024,256]{1,0:T(8,128)(2,1)S(1)}, bf16[1024,256]{1,0:T(8,128)(2,1)S(1)}, u32[]{:S(2)}, u32[]{:S(2)}) collective-permute-start(bf16[1024,256]{1,0:T(8,128)(2,1)S(1)} %slice_bitcast_fusion), channel_id=1, source_target_pairs={{0,8},{8,16},{16,24},{24,32},{32,40},{40,48},{48,56},{56,64},{64,7... | collective-permute-start | bytes 1572872 | tf_op jit(solution)/shard_map/ppermute | solution.py:26
  153.2 15.7 %collective-permute-start.1 = (bf16[1024,256]{1,0:T(8,128)(2,1)S(1)}, bf16[1024,256]{1,0:T(8,128)(2,1)S(1)}, u32[]{:S(2)}, u32[]{:S(2)}) collective-permute-start(bf16[1024,256]{1,0:T(8,128)(2,1)S(1)} %collective-permute-done), channel_id=1, source_target_pairs={{0,8},{8,16},{16,24},{24,32},{32,40},{40,48},{48,56},{56,64},{64,7... | collective-permute-start | bytes 1572872 | tf_op jit(solution)/shard_map/ppermute | solution.py:26
  168.9 14.8 %collective-permute-start.2 = (bf16[1024,256]{1,0:T(8,128)(2,1)S(1)}, bf16[1024,256]{1,0:T(8,128)(2,1)S(1)}, u32[]{:S(2)}, u32[]{:S(2)}) collective-permute-start(bf16[1024,256]{1,0:T(8,128)(2,1)S(1)} %collective-permute-done.1), channel_id=1, source_target_pairs={{0,8},{8,16},{16,24},{24,32},{32,40},{40,48},{48,56},{56,64},{64,7... | collective-permute-start | bytes 1572872 | tf_op jit(solution)/shard_map/ppermute | solution.py:26
  183.7 14.0 %collective-permute-start.3 = (bf16[1024,256]{1,0:T(8,128)(2,1)S(1)}, bf16[1024,256]{1,0:T(8,128)(2,1)S(1)}, u32[]{:S(2)}, u32[]{:S(2)}) collective-permute-start(bf16[1024,256]{1,0:T(8,128)(2,1)S(1)} %collective-permute-done.2), channel_id=1, source_target_pairs={{0,8},{8,16},{16,24},{24,32},{32,40},{40,48},{48,56},{56,64},{64,7... | collective-permute-start | bytes 1572872 | tf_op jit(solution)/shard_map/ppermute | solution.py:26
  197.7 13.1 %collective-permute-start.4 = (bf16[1024,256]{1,0:T(8,128)(2,1)S(1)}, bf16[1024,256]{1,0:T(8,128)(2,1)S(1)}, u32[]{:S(2)}, u32[]{:S(2)}) collective-permute-start(bf16[1024,256]{1,0:T(8,128)(2,1)S(1)} %collective-permute-done.3), channel_id=1, source_target_pairs={{0,8},{8,16},{16,24},{24,32},{32,40},{40,48},{48,56},{56,64},{64,7... | collective-permute-start | bytes 1572872 | tf_op jit(solution)/shard_map/ppermute | solution.py:26
  210.8 12.3 %collective-permute-start.5 = (bf16[1024,256]{1,0:T(8,128)(2,1)S(1)}, bf16[1024,256]{1,0:T(8,128)(2,1)S(1)}, u32[]{:S(2)}, u32[]{:S(2)}) collective-permute-start(bf16[1024,256]{1,0:T(8,128)(2,1)S(1)} %collective-permute-done.4), channel_id=1, source_target_pairs={{0,8},{8,16},{16,24},{24,32},{32,40},{40,48},{48,56},{56,64},{64,7... | collective-permute-start | bytes 1572872 | tf_op jit(solution)/shard_map/ppermute | solution.py:26
  223.1 11.4 %collective-permute-start.6 = (bf16[1024,256]{1,0:T(8,128)(2,1)S(1)}, bf16[1024,256]{1,0:T(8,128)(2,1)S(1)}, u32[]{:S(2)}, u32[]{:S(2)}) collective-permute-start(bf16[1024,256]{1,0:T(8,128)(2,1)S(1)} %collective-permute-done.5), channel_id=1, source_target_pairs={{0,8},{8,16},{16,24},{24,32},{32,40},{40,48},{48,56},{56,64},{64,7... | collective-permute-start | bytes 1572872 | tf_op jit(solution)/shard_map/ppermute | solution.py:26
  234.5 11.5 %collective-permute-start.7 = (bf16[1024,256]{1,0:T(8,128)(2,1)S(1)}, bf16[1024,256]{1,0:T(8,128)(2,1)S(1)}, u32[]{:S(2)}, u32[]{:S(2)}) collective-permute-start(bf16[1024,256]{1,0:T(8,128)(2,1)S(1)} %collective-permute-done.6), channel_id=1, source_target_pairs={{0,8},{8,16},{16,24},{24,32},{32,40},{40,48},{48,56},{56,64},{64,7... | collective-permute-start | bytes 1572872 | tf_op jit(solution)/shard_map/ppermute | solution.py:26
  253.7 251.1 %all-gather.10.cloned.1.call-start = ((), (), s32[]{:S(2)}) async-start(), calls=%async_computation.3 | async-start | bytes 2228224 | tf_op jit(solution)/shard_map/all_gather | solution.py:112
  253.8 8.1 %collective-permute-start.8 = (bf16[1024,256]{1,0:T(8,128)(2,1)S(1)}, bf16[1024,256]{1,0:T(8,128)(2,1)S(1)}, u32[]{:S(2)}, u32[]{:S(2)}) collective-permute-start(bf16[1024,256]{1,0:T(8,128)(2,1)S(1)} %slice_bitcast_fusion), channel_id=1, source_target_pairs={{8,0},{16,8},{24,16},{32,24},{40,32},{48,40},{56,48},{64,56},{72,6... | collective-permute-start | bytes 1572872 | tf_op jit(solution)/shard_map/ppermute | solution.py:28
  261.9 20.2 %collective-permute-start.9 = (bf16[1024,256]{1,0:T(8,128)(2,1)S(1)}, bf16[1024,256]{1,0:T(8,128)(2,1)S(1)}, u32[]{:S(2)}, u32[]{:S(2)}) collective-permute-start(bf16[1024,256]{1,0:T(8,128)(2,1)S(1)} %collective-permute-done.8), channel_id=1, source_target_pairs={{8,0},{16,8},{24,16},{32,24},{40,32},{48,40},{56,48},{64,56},{72,6... | collective-permute-start | bytes 1572872 | tf_op jit(solution)/shard_map/ppermute | solution.py:28
  282.0 12.8 %collective-permute-start.10 = (bf16[1024,256]{1,0:T(8,128)(2,1)S(1)}, bf16[1024,256]{1,0:T(8,128)(2,1)S(1)}, u32[]{:S(2)}, u32[]{:S(2)}) collective-permute-start(bf16[1024,256]{1,0:T(8,128)(2,1)S(1)} %collective-permute-done.9), channel_id=1, source_target_pairs={{8,0},{16,8},{24,16},{32,24},{40,32},{48,40},{56,48},{64,56},{72,6... | collective-permute-start | bytes 1572872 | tf_op jit(solution)/shard_map/ppermute | solution.py:28
  294.9 22.8 %collective-permute-start.11 = (bf16[1024,256]{1,0:T(8,128)(2,1)S(1)}, bf16[1024,256]{1,0:T(8,128)(2,1)S(1)}, u32[]{:S(2)}, u32[]{:S(2)}) collective-permute-start(bf16[1024,256]{1,0:T(8,128)(2,1)S(1)} %collective-permute-done.10), channel_id=1, source_target_pairs={{8,0},{16,8},{24,16},{32,24},{40,32},{48,40},{56,48},{64,56},{72,6... | collective-permute-start | bytes 1572872 | tf_op jit(solution)/shard_map/ppermute | solution.py:28
  317.6 26.2 %collective-permute-start.12 = (bf16[1024,256]{1,0:T(8,128)(2,1)S(1)}, bf16[1024,256]{1,0:T(8,128)(2,1)}, u32[]{:S(2)}, u32[]{:S(2)}) collective-permute-start(bf16[1024,256]{1,0:T(8,128)(2,1)S(1)} %collective-permute-done.11), channel_id=1, source_target_pairs={{8,0},{16,8},{24,16},{32,24},{40,32},{48,40},{56,48},{64,56},{72,6... | collective-permute-start | bytes 1572872 | tf_op jit(solution)/shard_map/ppermute | solution.py:28
  323.2 256.7 %reduce-scatter.2.cloned.1.call-start = ((), (), s32[]{:S(2)}) async-start(), calls=%async_computation.4 | async-start | bytes 9437184 | tf_op jit(solution)/shard_map/reduce_scatter | solution.py:113
  343.8 21.0 %collective-permute-start.13 = (bf16[1024,256]{1,0:T(8,128)(2,1)}, bf16[1024,256]{1,0:T(8,128)(2,1)}, u32[]{:S(2)}, u32[]{:S(2)}) collective-permute-start(bf16[1024,256]{1,0:T(8,128)(2,1)} %collective-permute-done.12), channel_id=1, source_target_pairs={{8,0},{16,8},{24,16},{32,24},{40,32},{48,40},{56,48},{64,56},{72,6... | collective-permute-start | bytes 1572872 | tf_op jit(solution)/shard_map/ppermute | solution.py:28
  364.8 17.1 %collective-permute-start.14 = (bf16[1024,256]{1,0:T(8,128)(2,1)}, bf16[1024,256]{1,0:T(8,128)(2,1)}, u32[]{:S(2)}, u32[]{:S(2)}) collective-permute-start(bf16[1024,256]{1,0:T(8,128)(2,1)} %collective-permute-done.13), channel_id=1, source_target_pairs={{8,0},{16,8},{24,16},{32,24},{40,32},{48,40},{56,48},{64,56},{72,6... | collective-permute-start | bytes 1572872 | tf_op jit(solution)/shard_map/ppermute | solution.py:28
  383.9 8.4 %copy-start.3 = (s32[2,4]{1,0:T(2,128)S(1)}, s32[2,4]{1,0:T(2,128)}, u32[]{:S(2)}) copy-start(s32[2,4]{1,0:T(2,128)} %add_add_fusion.1) | copy-start | bytes 100
  418.0 4.1 copy-start.2
  474.1 4.1 copy-start.2
  504.8 75.1 %copy-start.1 = (s32[128,16]{0,1:T(8,128)S(1)}, s32[128,16]{0,1:T(8,128)}, u32[]{:S(2)}) copy-start(s32[128,16]{0,1:T(8,128)} %param.11) | copy-start | bytes 24580
Sparse Core Ops, SparseCore 0:
  9.5 64.1 all-gather.7
  75.4 50.1 all-gather.5
  253.8 109.1 all-gather.11
  365.0 49.2 all-gather.9
  512.2 67.6 reduce-scatter.1
